TPU v7x, 32 devices: a whole 2x2x4 slice. The times are simulated.
32 devices in a mesh: ctx: 16 (over z, y, x), head: 2 (over core).
Axes of the slice: x: 2, y: 2, z: 4, core: 2. Of those that a mesh axis runs over, the one named last changes fastest.
Arguments:
- queries: bfloat16 [8192, 4, 4, 128], P('ctx', 'head')
- keys: bfloat16 [8192, 4, 128], P('ctx')
- values: bfloat16 [8192, 4, 128], P('ctx'), may hold values from -6 to 6
- output_gradient: bfloat16 [8192, 4, 4, 128], P('ctx', 'head'), may hold values from -6 to 6
- selected: int32 [16, 2], replicated, may hold values from 0 to 14, as said below
Outputs:
- attn_out: bfloat16 [8192, 4, 4, 128], P('ctx', 'head')
- grad_q: bfloat16 [8192, 4, 4, 128], P('ctx', 'head')
- grad_k: bfloat16 [8192, 4, 128], P('ctx', 'head')
- grad_v: bfloat16 [8192, 4, 128], P('ctx', 'head')
Inputs may be any that keep to these rules, and one draw needn't show every extreme that they name: selected[b, j] <= b for every block b; an entry equal to b selects no block; for b >= 2 the two entries of a row differ and both are below b.
All inputs are finite; a program needn't handle non-finite values.
Results may differ from a plain program's by a relative error of at most 0.011.
Values may be sent and summed in bfloat16 or wider, within the bound.
A program may use at most 128 MiB of HBM per device.

v0:
```python
import functools
import math

import jax
import jax.numpy as jnp
from jax import lax
from jax.experimental import pallas as pl
from jax.experimental.pallas import tpu as pltpu
from jax.sharding import PartitionSpec as P

F32 = jnp.float32
BF16 = jnp.bfloat16


def dot_nt(a, b):
    return lax.dot_general(a, b, (((1,), (1,)), ((), ())), preferred_element_type=F32)


def dot_nn(a, b):
    return lax.dot_general(a, b, (((1,), (0,)), ((), ())), preferred_element_type=F32)


def greet(blocks, halves):
    me, half = lax.axis_index("ctx"), lax.axis_index("head")
    barrier = pltpu.get_barrier_semaphore()

    @pl.loop(1, blocks)
    def _(i):
        pl.semaphore_signal(barrier, inc=1, device_id={"ctx": lax.rem(me + i, blocks), "head": half})

    for i in range(1, halves):
        pl.semaphore_signal(barrier, inc=1, device_id={"ctx": me, "head": lax.rem(half + i, halves)})
    pl.semaphore_wait(barrier, blocks - 1 + halves - 1)


def attend_tile(t, tile, scale, visible, q, do, keys, values, kt_ref, vt_ref, dk_ref, dv_ref):
    rows, size = keys.shape[1], keys.shape[2]
    factor = scale * math.log2(math.e)
    do_t = do.astype(F32).T
    do_tb = do_t.astype(BF16)
    q_tb = q.astype(F32).T.astype(BF16)
    counts = (rows, rows, (t + 1) * tile)
    scores, tops = [], []
    for j in range(3):
        s = dot_nn(keys[j, 0:counts[j], :], q_tb) * factor
        if j == 2:
            key_at = lax.broadcasted_iota(jnp.int32, s.shape, 0)
            query_at = lax.broadcasted_iota(jnp.int32, s.shape, 1) + t * tile
            s = jnp.where(key_at <= query_at, s, -jnp.inf)
        top = jnp.max(s, axis=0, keepdims=True)
        if j < 2:
            top = jnp.where(visible[j], top, -jnp.inf)
        scores.append(s)
        tops.append(top)
    top = jnp.maximum(jnp.maximum(tops[0], tops[1]), tops[2])
    total = jnp.zeros_like(top)
    weights = []
    for j in range(3):
        shift = jnp.where(visible[j], top, jnp.inf) if j < 2 else top
        e = jnp.exp2(scores[j] - shift)
        total = total + jnp.sum(e, axis=0, keepdims=True)
        weights.append(e)
    inverse = 1.0 / total
    out_t = jnp.zeros((size, tile), F32)
    lows, probs = [], []
    for j in range(3):
        p = weights[j] * inverse
        low = p.astype(BF16)
        probs.append(p)
        lows.append(low)
        out_t = out_t + dot_nn(vt_ref[:, j * rows:j * rows + counts[j]], low)
    out_low = out_t.astype(BF16).astype(F32)
    row_dot = jnp.sum(do_t * out_low, axis=0, keepdims=True)
    dq_t = jnp.zeros((size, tile), F32)
    for j in range(3):
        dp = dot_nn(values[j, 0:counts[j], :], do_tb)
        ds = (probs[j] * (dp - row_dot)).astype(BF16)
        dq_t = dq_t + dot_nn(kt_ref[:, j * rows:j * rows + counts[j]], ds)
        dk_ref[j, 0:counts[j], :] += dot_nn(ds, q)
        dv_ref[j, 0:counts[j], :] += dot_nn(lows[j], do)
    return out_low.T.astype(BF16), (dq_t * scale).T.astype(BF16)


def step_kernel(blocks, halves, tile, sel_ref, kv_ref, own_ref, q_ref, do_ref, grads_ref, oo_ref, dqo_ref,
                qv, dov, near, send, ks, vs, kt, vt, dk, dv, down, outv, dqv, dnear, arrived, home, ret,
                s1, r1, s2, r2, xs, xr, xl, b1, c1, b2, c2, ys, yr, yl, *held):
    me, half = lax.axis_index("ctx"), lax.axis_index("head")
    heads, group, rows, size = qv.shape
    part = group // halves
    piece = kv_ref.shape[2]
    scale = size ** -0.5
    visible = [sel_ref[me, j] < me for j in range(2)]
    here = {"ctx": me, "head": half}
    greet(blocks, halves)

    def send_all(make):
        @pl.loop(1, blocks)
        def _(i):
            make(lax.rem(me + i, blocks)).start()

    def spread(n):
        send_all(lambda peer: pltpu.make_async_remote_copy(
            kv_ref.at[n, peer], held[n].at[me], s1.at[n], r1.at[n], device_id={"ctx": peer, "head": half}))

    spread(0)

    moves = []
    for e, (src, dst) in enumerate(((q_ref, qv), (do_ref, dov))):
        place = dst.at[:, pl.ds(half * part, part)]
        for i in range(1, halves):
            other = lax.rem(half + i, halves)
            moves.append(pltpu.make_async_remote_copy(
                src.at[pl.ds(other * heads, heads)], place, xs.at[e, i - 1], xr.at[e, i - 1],
                device_id={"ctx": me, "head": other}))
        moves.append(pltpu.make_async_copy(src.at[pl.ds(half * heads, heads)], place, xl.at[e]))
    for move in moves:
        move.start()

    def fetch_first(n):
        return pltpu.make_async_remote_copy(
            kv_ref.at[n, pl.ds(0, blocks - 1)], held[n].at[pl.ds(0, blocks - 1)], s1.at[n], r1.at[n],
            device_id=here)

    def fetch_last(n):
        return pltpu.make_async_remote_copy(
            send.at[n, pl.ds(0, blocks - 1)], near.at[n, :, pl.ds(0, blocks - 1)], s2.at[n], r2.at[n],
            device_id=here)

    def relay(n):
        held[n][me] = kv_ref[n, me]
        fetch_first(n).wait_recv()

        @pl.loop(0, blocks)
        def _(dest):
            for j in range(2):
                send[n, dest, j] = held[n][sel_ref[dest, j]]

        send_all(lambda dest: pltpu.make_async_remote_copy(
            send.at[n, dest], near.at[n, :, me], s2.at[n], r2.at[n], device_id={"ctx": dest, "head": half}))
        if n + 1 < heads:
            spread(n + 1)
        for j in range(2):
            near[n, j, me] = held[n][sel_ref[me, j]]

    relay(0)

    for move in moves:
        move.wait()

    def back_first(n):
        return pltpu.make_async_remote_copy(
            dnear.at[n, :, pl.ds(0, blocks - 1)], arrived.at[n, pl.ds(0, blocks - 1)], b1.at[n], c1.at[n],
            device_id=here)

    def back_last(n):
        return pltpu.make_async_remote_copy(
            home.at[n, pl.ds(0, blocks - 1)], ret.at[n, pl.ds(0, blocks - 1)], b2.at[n], c2.at[n],
            device_id=here)

    together = math.gcd(4, blocks)

    def collect(n):
        back_first(n).wait_recv()

        def deliver(i):
            dest = lax.rem(me + i, blocks)
            pltpu.make_async_remote_copy(
                home.at[n, dest], ret.at[n, me], b2.at[n], c2.at[n],
                device_id={"ctx": dest, "head": half}).start()

        @pl.loop(1, blocks + 1)
        def _(i):
            s = lax.rem(me + i, blocks)

            def add(c, total):
                for k in range(together):
                    b = c * together + k
                    for j in range(2):
                        mine = ((sel_ref[b, j] == s) & (b > s)).astype(F32)
                        total = total + arrived[n, b, j].astype(F32) * mine
                return total

            total = lax.fori_loop((s + 1) // together, blocks // together, add, jnp.zeros((piece, size), F32))
            home[n, s] = total.astype(BF16)

            @pl.when(i > 1)
            def _():
                deliver(i - 1)

        ret[n, me] = home[n, me]

    def results(n):
        made = []
        for e, (src, dst) in enumerate(((outv, oo_ref), (dqv, dqo_ref))):
            place = dst.at[half * heads + n]
            for i in range(1, halves):
                other = lax.rem(half + i, halves)
                made.append(pltpu.make_async_remote_copy(
                    src.at[n, pl.ds(other * part, part)], place, ys.at[n, e, i - 1], yr.at[n, e, i - 1],
                    device_id={"ctx": me, "head": other}))
            made.append(pltpu.make_async_copy(src.at[n, pl.ds(half * part, part)], place, yl.at[n, e]))
        return made

    def join(x):
        if piece % 16 == 0:
            return x.reshape(rows, size)
        return x.astype(F32).reshape(rows, size).astype(BF16)

    pieces = blocks // 2

    @pl.loop(0, heads * group)
    def _(at):
        n = at // group
        g = at % group

        @pl.when(g == 0)
        def _():
            fetch_last(n).wait_recv()
            for j in range(3):
                if j < 2:
                    k, v = join(near[n, j, 0:pieces]), join(near[n, j, pieces:2 * pieces])
                else:
                    k, v = own_ref[n, 0], own_ref[n, 1]
                ks[j] = k
                vs[j] = v
                kt[:, j * rows:(j + 1) * rows] = k.astype(F32).T.astype(BF16)
                vt[:, j * rows:(j + 1) * rows] = v.astype(F32).T.astype(BF16)
            dk[...] = jnp.zeros_like(dk)
            dv[...] = jnp.zeros_like(dv)

        for t in range(rows // tile):
            span = slice(t * tile, (t + 1) * tile)
            out, dq = attend_tile(t, tile, scale, visible, qv[n, g, span, :], dov[n, g, span, :],
                                  ks, vs, kt, vt, dk, dv)
            outv[n, g, span, :] = out
            dqv[n, g, span, :] = dq

        for m in range(1, heads):
            @pl.when(at == (m - 1) * group)
            def _(m=m):
                relay(m)

        @pl.when(g == group - 1)
        def _():
            for j in range(2):
                dnear[n, j, 0:pieces] = (dk[j] * scale).reshape(pieces, piece, size).astype(BF16)
                dnear[n, j, pieces:2 * pieces] = dv[j].reshape(pieces, piece, size).astype(BF16)
            down[n, 0:pieces] = (dk[2] * scale).reshape(pieces, piece, size)
            down[n, pieces:2 * pieces] = dv[2].reshape(pieces, piece, size)
            send_all(lambda peer: pltpu.make_async_remote_copy(
                dnear.at[n, :, peer], arrived.at[n, me], b1.at[n], c1.at[n],
                device_id={"ctx": peer, "head": half}))
            for j in range(2):
                arrived[n, me, j] = dnear[n, j, me]
            for move in results(n):
                move.start()

        @pl.when((n > 0) & (g == group - 2))
        def _():
            collect(n - 1)

    collect(heads - 1)
    for n in range(heads):
        fetch_first(n).wait_send()
        fetch_last(n).wait_send()
        back_first(n).wait_send()
        for move in results(n):
            move.wait()
    for n in range(heads):
        back_last(n).wait_send()
        back_last(n).wait_recv()
        grads_ref[n] = (ret[n].astype(F32) + down[n]).astype(BF16)


def step(selected, kv, own, q, do, blocks, halves):
    heads, _, piece, size = kv.shape
    full, part, rows, _ = q.shape
    group = part * halves
    tile = min(256, rows)
    near = pl.BlockSpec(memory_space=pltpu.VMEM)
    far = pl.BlockSpec(memory_space=pl.ANY)
    dma = pltpu.SemaphoreType.DMA
    vmem = pltpu.VMEM
    return pl.pallas_call(
        functools.partial(step_kernel, blocks, halves, tile),
        in_specs=[pl.BlockSpec(memory_space=pltpu.SMEM), near, near, far, far],
        out_specs=[near, far, far],
        out_shape=[jax.ShapeDtypeStruct(kv.shape, BF16), jax.ShapeDtypeStruct(q.shape, BF16),
                   jax.ShapeDtypeStruct(q.shape, BF16)],
        scratch_shapes=[
            vmem((heads, group, rows, size), BF16),
            vmem((heads, group, rows, size), BF16),
            vmem((heads, 2, blocks, piece, size), BF16),
            vmem((heads, blocks, 2, piece, size), BF16),
            vmem((3, rows, size), BF16),
            vmem((3, rows, size), BF16),
            vmem((size, 3 * rows), BF16),
            vmem((size, 3 * rows), BF16),
            vmem((3, rows, size), F32),
            vmem((3, rows, size), F32),
            vmem((heads, blocks, piece, size), F32),
            vmem((heads, group, rows, size), BF16),
            vmem((heads, group, rows, size), BF16),
            vmem((heads, 2, blocks, piece, size), BF16),
            vmem((heads, blocks, 2, piece, size), BF16),
            vmem((heads, blocks, piece, size), BF16),
            vmem((heads, blocks, piece, size), BF16),
            dma((heads,)), dma((heads,)), dma((heads,)), dma((heads,)),
            dma((2, halves - 1)), dma((2, halves - 1)), dma((2,)),
            dma((heads,)), dma((heads,)), dma((heads,)), dma((heads,)),
            dma((heads, 2, halves - 1)), dma((heads, 2, halves - 1)), dma((heads, 2)),
        ] + [vmem((blocks, piece, size), BF16)] * heads,
        compiler_params=pltpu.CompilerParams(collective_id=0, has_side_effects=True,
                                             vmem_limit_bytes=56 * 2**20),
    )(selected, kv, own, q, do)


def on_device(queries, keys, values, output_gradient, selected):
    rows, kv_count, size = keys.shape
    blocks, halves = lax.axis_size("ctx"), lax.axis_size("head")
    own_heads = kv_count // halves
    half = lax.axis_index("head")
    piece = 2 * rows // blocks
    own = jnp.stack([keys, values])
    own = lax.dynamic_slice_in_dim(own, half * own_heads, own_heads, 2)
    own = jnp.transpose(own, (2, 0, 1, 3))
    q, do = jnp.transpose(queries, (2, 1, 0, 3)), jnp.transpose(output_gradient, (2, 1, 0, 3))
    grads, out, dq = step(selected, own.reshape(own_heads, blocks, piece, size), own, q, do, blocks, halves)
    grads = jnp.transpose(grads.reshape(own.shape), (1, 2, 0, 3))
    return jnp.transpose(out, (2, 1, 0, 3)), jnp.transpose(dq, (2, 1, 0, 3)), grads[0], grads[1]


def solution(mesh):
    return jax.shard_map(
        on_device,
        mesh=mesh,
        in_specs=(
            P("ctx", "head", None, None),
            P("ctx", None, None),
            P("ctx", None, None),
            P("ctx", "head", None, None),
            P(),
        ),
        out_specs=(
            P("ctx", "head", None, None),
            P("ctx", "head", None, None),
            P("ctx", "head", None),
            P("ctx", "head", None),
        ),
        check_vma=False,
    )
```

profile of v0, /device:TPU:0, one launch (start us, length us, event | category | flops | bytes accessed | tf_op | source)
XLA Modules:
  0.0 98.6 jit_solution(6268071317288070542)
XLA Ops:
  0.6 0.0 copy-start.4
  0.6 0.7 copy-done.4
  1.3 0.7 copy.13.sel_ref
  2.0 1.3 %copy_bitcast_fusion.3 = (bf16[1,512,4,128]{3,1,0,2:T(8,128)(2,1)S(1)}, bf16[1,512,4,128]{3,1,0,2:T(8,128)(2,1)S(1)}) fusion(bf16[512,4,128]{2,1,0:T(4,128)(2,1)} %param.7, bf16[512,4,128]{2,1,0:T(4,128)(2,1)} %param.6), kind=kLoop, calls=%fused_computation.6 | loop fusion | bytes 2097152 | tf_op jit(solution)/shard_map/stack | solution.py:324
  3.3 0.0 copy-start.2
  3.3 0.9 fusion.1.own_ref
  4.2 0.0 copy-start.1
  4.2 0.9 fusion
  5.1 0.0 copy-done.2
  5.1 0.6 copy-done.1
  5.7 1.7 %copy_bitcast_fusion = (bf16[4,2,512,128]{3,2,1,0:T(8,128)(2,1)}, bf16[4,2,512,128]{3,2,1,0:T(8,128)(2,1)}) fusion(bf16[512,2,4,128]{3,2,1,0:T(4,128)(2,1)S(1)} %copy-done.1, bf16[512,2,4,128]{3,2,1,0:T(4,128)(2,1)S(1)} %copy-done.2), kind=kLoop, calls=%fused_computation.2 | loop fusion | bytes 4194304 | tf_op jit(solution)/shard_map/transpose | solution.py:327
  7.4 84.6 %shard_map.84 = (bf16[2,16,64,128]{3,2,1,0:T(8,128)(2,1)}, bf16[4,2,512,128]{3,2,1,0:T(8,128)(2,1)}, bf16[4,2,512,128]{3,2,1,0:T(8,128)(2,1)}) custom-call(s32[16,2]{1,0:T(8,128)} %copy.13.sel_ref, bf16[2,16,64,128]{3,2,1,0:T(8,128)(2,1)} %bitcast.23, bf16[2,2,512,128]{3,2,1,0:T(8,128)(2,1)} %fusion.1.own_ref, ...), custom_call_target="tpu_custom_call" | custom-call | tf_op jit(solution)/shard_map/pallas_call | solution.py:284
  92.0 0.0 copy-start
  92.0 3.1 %copy.15 = bf16[512,2,4,128]{3,2,1,0:T(4,128)(2,1)} copy(bf16[512,2,4,128]{3,0,1,2:T(8,128)(2,1)} %bitcast.25) | data formatting | bytes 2097152
  95.1 0.0 copy-done
  95.1 0.0 copy-start.3
  95.1 1.8 %copy.16 = bf16[512,2,4,128]{3,2,1,0:T(4,128)(2,1)} copy(bf16[512,2,4,128]{3,0,1,2:T(8,128)(2,1)S(1)} %bitcast.24) | data formatting | bytes 2097152
  96.9 0.0 copy-done.3
  96.9 0.5 copy.22
  97.5 1.2 %slice_bitcast_fusion = (bf16[512,2,128]{2,1,0:T(2,128)(2,1)}, bf16[512,2,128]{2,1,0:T(2,128)(2,1)}) fusion(bf16[2,512,2,128]{3,2,1,0:T(2,128)(2,1)S(1)} %bitcast.22), kind=kLoop, calls=%fused_computation.8 | loop fusion | bytes 1048576 | tf_op jit(solution)/shard_map/squeeze | solution.py:330
Async XLA Ops:
  0.6 0.7 copy-start.4
  3.3 1.7 %copy-start.2 = (bf16[512,2,4,128]{3,2,1,0:T(4,128)(2,1)S(1)}, bf16[512,2,4,128]{3,2,1,0:T(4,128)(2,1)}, u32[]{:S(2)}) copy-start(bf16[512,2,4,128]{3,2,1,0:T(4,128)(2,1)} %param.5) | copy-start | bytes 3145732
  4.2 1.5 %copy-start.1 = (bf16[512,2,4,128]{3,2,1,0:T(4,128)(2,1)S(1)}, bf16[512,2,4,128]{3,2,1,0:T(4,128)(2,1)}, u32[]{:S(2)}) copy-start(bf16[512,2,4,128]{3,2,1,0:T(4,128)(2,1)} %param.8) | copy-start | bytes 3145732
  92.0 3.1 %copy-start = (bf16[4,2,512,128]{3,2,1,0:T(8,128)(2,1)S(1)}, bf16[4,2,512,128]{3,2,1,0:T(8,128)(2,1)}, u32[]{:S(2)}) copy-start(bf16[4,2,512,128]{3,2,1,0:T(8,128)(2,1)} %get-tuple-element.8) | copy-start | bytes 3145732
  95.1 1.8 %copy-start.3 = (bf16[2,16,64,128]{3,2,1,0:T(8,128)(2,1)S(1)}, bf16[2,16,64,128]{3,2,1,0:T(8,128)(2,1)}, u32[]{:S(2)}) copy-start(bf16[2,16,64,128]{3,2,1,0:T(8,128)(2,1)} %get-tuple-element.9) | copy-start | bytes 1572868
where the time goes:
time: 98.9 us; the launch traced here: 98.6 us
  Pallas kernels  84.6 us (86%)
  local copies, waits for them, and re-layouts  11.6 us (12%)
  other arithmetic  1.72 us (2%)
    pallas_call x1, Pallas kernels, step(): pl.pallas_call(functools.partial(step_kernel, blocks, halves, tile), in_s...  84.6 us
    unnamed x13, local copies, waits for them, and re-layouts  6.87 us

commit v1 on v0

v1 whole, which is shorter than its diff:
```python
import functools
import math

import jax
import jax.numpy as jnp
from jax import lax
from jax.experimental import pallas as pl
from jax.experimental.pallas import tpu as pltpu
from jax.sharding import PartitionSpec as P

F32 = jnp.float32
BF16 = jnp.bfloat16
CHUNKS = 2


def dot_nn(a, b):
    return lax.dot_general(a, b, (((1,), (0,)), ((), ())), preferred_element_type=F32)


def greet(blocks, halves):
    me, half = lax.axis_index("ctx"), lax.axis_index("head")
    barrier = pltpu.get_barrier_semaphore()

    @pl.loop(1, blocks)
    def _(i):
        pl.semaphore_signal(barrier, inc=1, device_id={"ctx": lax.rem(me + i, blocks), "head": half})

    for i in range(1, halves):
        pl.semaphore_signal(barrier, inc=1, device_id={"ctx": me, "head": lax.rem(half + i, halves)})
    pl.semaphore_wait(barrier, blocks - 1 + halves - 1)


def flip(x):
    return x.astype(F32).T.astype(BF16)


def step_kernel(blocks, halves, sel_ref, kv_ref, own_ref, q_ref, do_ref, grads_ref, oo_ref, dqo_ref,
                qv, dov, qt, dot, near, send, ks, vs, kt, vt, probs, dots, dqt, dk, dv, dko, dvo, down, outv, dqv,
                dnear, arrived, home, ret,
                s1, r1, s2, r2, xs, xr, xl, b1, c1, b2, c2, ys, yr, yl, *held):
    me, half = lax.axis_index("ctx"), lax.axis_index("head")
    heads, group, rows, size = qv.shape
    part = group // halves
    side_blocks, piece = kv_ref.shape[1], kv_ref.shape[2]
    units = heads * CHUNKS
    keys = rows // CHUNKS
    tile = rows // 2
    side, col = me // side_blocks, lax.rem(me, side_blocks)
    base = side * side_blocks
    lower, upper = side == 0, side > 0
    scale = size ** -0.5
    factor = scale * math.log2(math.e)
    visible = [sel_ref[me, j] < me for j in range(2)]
    here = {"ctx": me, "head": half}
    greet(blocks, halves)

    def near_all(make):
        @pl.loop(1, side_blocks)
        def _(i):
            make(lax.rem(col + i, side_blocks)).start()

    def far_all(make):
        @pl.loop(0, side_blocks)
        def _(i):
            make(lax.rem(col + i, side_blocks)).start()

    def scatter(u, first):
        return lambda d: pltpu.make_async_remote_copy(
            kv_ref.at[u, d], held[u].at[me], s1.at[u], r1.at[u], device_id={"ctx": first + d, "head": half})

    for u in range(units):
        @pl.when(lower)
        def _(u=u):
            far_all(scatter(u, side_blocks))

        near_all(scatter(u, base))

    moves = []
    for e, (src, dst) in enumerate(((q_ref, qv), (do_ref, dov))):
        place = dst.at[:, pl.ds(half * part, part)]
        for i in range(1, halves):
            other = lax.rem(half + i, halves)
            moves.append(pltpu.make_async_remote_copy(
                src.at[pl.ds(other * heads, heads)], place, xs.at[e, i - 1], xr.at[e, i - 1],
                device_id={"ctx": me, "head": other}))
        moves.append(pltpu.make_async_copy(src.at[pl.ds(half * heads, heads)], place, xl.at[e]))
    for move in moves:
        move.start()

    def fetch_first(u, count):
        span = pl.ds(0, count)
        return pltpu.make_async_remote_copy(
            held[u].at[span], held[u].at[span], s1.at[u], r1.at[u], device_id=here)

    def fetch_last(u):
        span = pl.ds(0, side_blocks - 1)
        return pltpu.make_async_remote_copy(
            send.at[u, span], near.at[u, :, span], s2.at[u], r2.at[u], device_id=here)

    def relay(u):
        held[u][me] = kv_ref[u, col]

        @pl.when(lower)
        def _():
            fetch_first(u, side_blocks - 1).wait_recv()

        @pl.when(upper)
        def _():
            fetch_first(u, blocks - 1).wait_recv()

        @pl.loop(0, side_blocks)
        def _(d):
            for j in range(2):
                send[u, d, j] = held[u][sel_ref[base + d, j]]

        near_all(lambda d: pltpu.make_async_remote_copy(
            send.at[u, d], near.at[u, :, col], s2.at[u], r2.at[u], device_id={"ctx": base + d, "head": half}))
        for j in range(2):
            near[u, j, col] = held[u][sel_ref[me, j]]

    def back_first(u):
        span = pl.ds(0, side_blocks - 1)
        return pltpu.make_async_remote_copy(
            dnear.at[u, :, span], arrived.at[u, span], b1.at[u], c1.at[u], device_id=here)

    def back_last(u, count):
        span = pl.ds(0, count)
        return pltpu.make_async_remote_copy(
            home.at[u, span], home.at[u, span], b2.at[u], c2.at[u], device_id=here)

    together = math.gcd(4, side_blocks)

    def collect(u):
        back_first(u).wait_recv()

        def total_of(s, first):
            def add(c, total):
                for k in range(together):
                    d = c * together + k
                    b = base + d
                    for j in range(2):
                        mine = ((sel_ref[b, j] == s) & (b > s)).astype(F32)
                        total = total + arrived[u, d, j].astype(F32) * mine
                return total

            total = lax.fori_loop(first, side_blocks // together, add, jnp.zeros((piece, size), F32))
            home[u, s] = total.astype(BF16)

        def deliver(s):
            pltpu.make_async_remote_copy(
                home.at[u, s], ret.at[u, side, col], b2.at[u], c2.at[u],
                device_id={"ctx": s, "head": half}).start()

        @pl.when(upper)
        def _():
            @pl.loop(0, side_blocks)
            def _(i):
                total_of(lax.rem(col + i, side_blocks), 0)

                @pl.when(i > 0)
                def _():
                    deliver(lax.rem(col + i - 1, side_blocks))

            deliver(lax.rem(col + side_blocks - 1, side_blocks))

        @pl.loop(1, side_blocks + 1)
        def _(i):
            d = lax.rem(col + i, side_blocks)
            total_of(base + d, (d + 1) // together)

            @pl.when(i > 1)
            def _():
                deliver(base + lax.rem(col + i - 1, side_blocks))

        ret[u, side, col] = home[u, me]

    def results(n, e):
        src, dst = ((outv, oo_ref), (dqv, dqo_ref))[e]
        made = []
        place = dst.at[half * heads + n]
        for i in range(1, halves):
            other = lax.rem(half + i, halves)
            made.append(pltpu.make_async_remote_copy(
                src.at[n, pl.ds(other * part, part)], place, ys.at[n, e, i - 1], yr.at[n, e, i - 1],
                device_id={"ctx": me, "head": other}))
        made.append(pltpu.make_async_copy(src.at[n, pl.ds(half * part, part)], place, yl.at[n, e]))
        return made

    def join(x):
        if piece % 16 == 0:
            return x.reshape(keys, size)
        return x.astype(F32).reshape(keys, size).astype(BF16)

    pieces = side_blocks // 2

    def place_keys(n, j, k, key, value):
        ks[n, j, k * keys:(k + 1) * keys] = key
        vs[n, j, k * keys:(k + 1) * keys] = value
        kt[n, j, k] = flip(key)
        vt[n, :, j * rows + k * keys:j * rows + (k + 1) * keys] = flip(value)

    def outputs(n, g):
        for t in range(2):
            span = slice(t * tile, (t + 1) * tile)
            counts = (rows, rows, (t + 1) * tile)
            q_t = qt[n, g, :, span]
            scores, tops = [], []
            for j in range(3):
                s = dot_nn(ks[n, j, 0:counts[j], :], q_t) * factor
                if j == 2:
                    key_at = lax.broadcasted_iota(jnp.int32, s.shape, 0)
                    query_at = lax.broadcasted_iota(jnp.int32, s.shape, 1) + t * tile
                    s = jnp.where(key_at <= query_at, s, -jnp.inf)
                top = jnp.max(s, axis=0, keepdims=True)
                if j < 2:
                    top = jnp.where(visible[j], top, -jnp.inf)
                scores.append(s)
                tops.append(top)
            top = jnp.maximum(jnp.maximum(tops[0], tops[1]), tops[2])
            total = jnp.zeros_like(top)
            weights = []
            for j in range(3):
                shift = jnp.where(visible[j], top, jnp.inf) if j < 2 else top
                e = jnp.exp2(scores[j] - shift)
                total = total + jnp.sum(e, axis=0, keepdims=True)
                weights.append(e)
            inverse = 1.0 / total
            out_t = jnp.zeros((size, tile), F32)
            for j in range(3):
                low = (weights[j] * inverse).astype(BF16)
                probs[n, g, j * rows:j * rows + counts[j], span] = low
                out_t = out_t + dot_nn(vt[n, :, j * rows:j * rows + counts[j]], low)
            out_low = out_t.astype(BF16).astype(F32)
            dots[n, g, :, span] = jnp.sum(dot[n, g, :, span].astype(F32) * out_low, axis=0, keepdims=True)
            outv[n, g, span, :] = out_low.T.astype(BF16)

    def gradients(n, g, low, key_t, value, span, dk_at, dv_at):
        dp = dot_nn(value, dot[n, g, :, span])
        ds = (low.astype(F32) * (dp - dots[n, g, :, span])).astype(BF16)
        dk_at[...] += dot_nn(ds, qv[n, g, span, :])
        dv_at[...] += dot_nn(low, dov[n, g, span, :])
        return dot_nn(key_t, ds)

    def chunk(n, k, g):
        every = slice(0, rows)
        total = jnp.zeros((size, rows), F32)
        for j in range(2):
            at = pl.multiple_of(k * keys, keys)
            low = probs[n, g, pl.ds(pl.multiple_of(j * rows + k * keys, keys), keys), :]
            total = total + gradients(n, g, low, kt[n, j, k], vs[n, j, pl.ds(at, keys), :], every,
                                      dk.at[j], dv.at[j])

        @pl.when(k == 0)
        def _():
            dqt[n, g] = total

        @pl.when(k > 0)
        def _():
            dqt[n, g] += total

    def own_chunk(n, g):
        total = dqt[n, g]
        tails = []
        for k in range(CHUNKS):
            span = slice(k * keys, rows)
            low = probs[n, g, 2 * rows + k * keys:2 * rows + (k + 1) * keys, span]
            at = slice(k * keys, (k + 1) * keys)
            tails.append(gradients(n, g, low, kt[n, 2, k], vs[n, 2, at, :], span, dko.at[at], dvo.at[at]))
        for t in range(CHUNKS):
            span = slice(t * keys, (t + 1) * keys)
            dq = total[:, span]
            for k in range(t + 1):
                dq = dq + tails[k][:, (t - k) * keys:(t - k + 1) * keys]
            dqv[n, g, span, :] = (dq * scale).T.astype(BF16)

    for n in range(heads):
        for k in range(CHUNKS):
            span = slice(k * keys, (k + 1) * keys)
            place_keys(n, 2, k, own_ref[n, 0, span], own_ref[n, 1, span])

    for move in moves:
        move.wait()

    @pl.loop(0, heads * group)
    def _(at):
        n, g = at // group, lax.rem(at, group)
        qt[n, g] = flip(qv[n, g])
        dot[n, g] = flip(dov[n, g])

    for u in range(CHUNKS):
        relay(u)

    @pl.loop(0, heads)
    def _(n):
        for k in range(CHUNKS):
            u = n * CHUNKS + k
            fetch_last(u).wait_recv()
            for j in range(2):
                place_keys(n, j, k, join(near[u, j, 0:pieces]), join(near[u, j, pieces:2 * pieces]))

        @pl.loop(0, group)
        def _(g):
            outputs(n, g)
            for m in range(1, heads):
                for k in range(CHUNKS):
                    @pl.when((n == m - 1) & (g == k * (group - 1)))
                    def _(m=m, k=k):
                        relay(m * CHUNKS + k)

            @pl.when((n > 0) & (lax.rem(g, 2) == 1))
            def _():
                collect((n - 1) * CHUNKS + g // 2)

        for move in results(n, 0):
            move.start()

        @pl.loop(0, CHUNKS * group)
        def _(at):
            k, g = at // group, lax.rem(at, group)
            u = n * CHUNKS + k

            @pl.when(g == 0)
            def _():
                dk[...] = jnp.zeros_like(dk)
                dv[...] = jnp.zeros_like(dv)

            chunk(n, k, g)

            @pl.when(g == group - 1)
            def _():
                for j in range(2):
                    dnear[u, j, 0:pieces] = (dk[j] * scale).reshape(pieces, piece, size).astype(BF16)
                    dnear[u, j, pieces:2 * pieces] = dv[j].reshape(pieces, piece, size).astype(BF16)
                near_all(lambda d: pltpu.make_async_remote_copy(
                    dnear.at[u, :, d], arrived.at[u, col], b1.at[u], c1.at[u],
                    device_id={"ctx": base + d, "head": half}))
                for j in range(2):
                    arrived[u, col, j] = dnear[u, j, col]

    @pl.loop(0, heads * group)
    def _(at):
        n, g = at // group, lax.rem(at, group)

        @pl.when(g == 0)
        def _():
            dko[...] = jnp.zeros_like(dko)
            dvo[...] = jnp.zeros_like(dvo)

        own_chunk(n, g)

        for k in range(CHUNKS):
            @pl.when(at == (1 + 4 * k))
            def _(k=k):
                collect((heads - 1) * CHUNKS + k)

        @pl.when(g == group - 1)
        def _():
            for k in range(CHUNKS):
                u = n * CHUNKS + k
                span = slice(k * keys, (k + 1) * keys)
                down[u, 0:pieces] = (dko[span] * scale).reshape(pieces, piece, size)
                down[u, pieces:2 * pieces] = dvo[span].reshape(pieces, piece, size)
            for move in results(n, 1):
                move.start()

    for u in range(units):
        fetch_last(u).wait_send()
        back_first(u).wait_send()
    for n in range(heads):
        for e in range(2):
            for move in results(n, e):
                move.wait()

    @pl.when(lower)
    def _():
        for u in range(units):
            fetch_first(u, blocks - 1).wait_send()
            back_last(u, side_blocks - 1).wait_send()
            back_last(u, blocks - 1).wait_recv()
            grads_ref[u] = (ret[u, 1].astype(F32) + ret[u, 0].astype(F32) + down[u]).astype(BF16)

    @pl.when(upper)
    def _():
        for u in range(units):
            fetch_first(u, side_blocks - 1).wait_send()
            back_last(u, blocks - 1).wait_send()
            back_last(u, side_blocks - 1).wait_recv()
            grads_ref[u] = (ret[u, 1].astype(F32) + down[u]).astype(BF16)


def step(selected, kv, own, q, do, blocks, halves):
    units, side_blocks, piece, size = kv.shape
    heads = units // CHUNKS
    full, part, rows, _ = q.shape
    group = part * halves
    keys = rows // CHUNKS
    near = pl.BlockSpec(memory_space=pltpu.VMEM)
    far = pl.BlockSpec(memory_space=pl.ANY)
    dma = pltpu.SemaphoreType.DMA
    vmem = pltpu.VMEM
    return pl.pallas_call(
        functools.partial(step_kernel, blocks, halves),
        in_specs=[pl.BlockSpec(memory_space=pltpu.SMEM), near, near, far, far],
        out_specs=[near, far, far],
        out_shape=[jax.ShapeDtypeStruct(kv.shape, BF16), jax.ShapeDtypeStruct(q.shape, BF16),
                   jax.ShapeDtypeStruct(q.shape, BF16)],
        scratch_shapes=[
            vmem((heads, group, rows, size), BF16),
            vmem((heads, group, rows, size), BF16),
            vmem((heads, group, size, rows), BF16),
            vmem((heads, group, size, rows), BF16),
            vmem((units, 2, side_blocks, piece, size), BF16),
            vmem((units, side_blocks, 2, piece, size), BF16),
            vmem((heads, 3, rows, size), BF16),
            vmem((heads, 3, rows, size), BF16),
            vmem((heads, 3, CHUNKS, size, keys), BF16),
            vmem((heads, size, 3 * rows), BF16),
            vmem((heads, group, 3 * rows, rows), BF16),
            vmem((heads, group, 1, rows), F32),
            vmem((heads, group, size, rows), F32),
            vmem((2, keys, size), F32),
            vmem((2, keys, size), F32),
            vmem((rows, size), F32),
            vmem((rows, size), F32),
            vmem((units, side_blocks, piece, size), F32),
            vmem((heads, group, rows, size), BF16),
            vmem((heads, group, rows, size), BF16),
            vmem((units, 2, side_blocks, piece, size), BF16),
            vmem((units, side_blocks, 2, piece, size), BF16),
            vmem((units, blocks, piece, size), BF16),
            vmem((units, 2, side_blocks, piece, size), BF16),
            dma((units,)), dma((units,)), dma((units,)), dma((units,)),
            dma((2, halves - 1)), dma((2, halves - 1)), dma((2,)),
            dma((units,)), dma((units,)), dma((units,)), dma((units,)),
            dma((heads, 2, halves - 1)), dma((heads, 2, halves - 1)), dma((heads, 2)),
        ] + [vmem((blocks, piece, size), BF16)] * units,
        compiler_params=pltpu.CompilerParams(collective_id=0, has_side_effects=True,
                                             vmem_limit_bytes=56 * 2**20),
    )(selected, kv, own, q, do)


def on_device(queries, keys, values, output_gradient, selected):
    rows, kv_count, size = keys.shape
    blocks, halves = lax.axis_size("ctx"), lax.axis_size("head")
    own_heads = kv_count // halves
    half = lax.axis_index("head")
    side_blocks = blocks // 2
    piece = 2 * rows // (CHUNKS * side_blocks)
    own = jnp.stack([keys, values])
    own = lax.dynamic_slice_in_dim(own, half * own_heads, own_heads, 2)
    own = jnp.transpose(own, (2, 0, 1, 3))
    cut = own.reshape(own_heads, 2, CHUNKS, rows // CHUNKS, size)
    cut = jnp.transpose(cut, (0, 2, 1, 3, 4)).reshape(own_heads * CHUNKS, side_blocks, piece, size)
    q, do = jnp.transpose(queries, (2, 1, 0, 3)), jnp.transpose(output_gradient, (2, 1, 0, 3))
    grads, out, dq = step(selected, cut, own, q, do, blocks, halves)
    grads = grads.reshape(own_heads, CHUNKS, 2, rows // CHUNKS, size)
    grads = jnp.transpose(grads, (2, 1, 3, 0, 4)).reshape(2, rows, own_heads, size)
    return jnp.transpose(out, (2, 1, 0, 3)), jnp.transpose(dq, (2, 1, 0, 3)), grads[0], grads[1]


def solution(mesh):
    return jax.shard_map(
        on_device,
        mesh=mesh,
        in_specs=(
            P("ctx", "head", None, None),
            P("ctx", None, None),
            P("ctx", None, None),
            P("ctx", "head", None, None),
            P(),
        ),
        out_specs=(
            P("ctx", "head", None, None),
            P("ctx", "head", None, None),
            P("ctx", "head", None),
            P("ctx", "head", None),
        ),
        check_vma=False,
    )
```

time: 98.9 us -> 94.4 us (0.954)
  Pallas kernels: 84.6 us -> 79.6 us
  local copies, waits for them, and re-layouts: 11.6 us -> 12.9 us
    pallas_call x1, Pallas kernels: 84.6 us -> 79.6 us  [step(): pl.pallas_call(functools.partial(step_kernel, blocks, halves), in_specs=[...]
    slice x0 -> x3, local copies, waits for them, and re-layouts: none -> 1.98 us  [the longest x2 1.01 us: on_device(): grads[1]]
    squeeze x1 -> x0, local copies, waits for them, and re-layouts: 1.15 us -> none  [on_device(): grads[1]]
where the time goes in v1:
time: 94.4 us; the launch traced here: 94.1 us
  Pallas kernels  79.6 us (84%)
  local copies, waits for them, and re-layouts  12.9 us (14%)
    pallas_call x1, Pallas kernels, step(): pl.pallas_call(functools.partial(step_kernel, blocks, halves), in_specs=[...  79.6 us
    unnamed x13, local copies, waits for them, and re-layouts  7.06 us

profile of v1, /device:TPU:0, one launch (start us, length us, event | category | flops | bytes accessed | tf_op | source)
XLA Modules:
  0.0 94.1 jit_solution(6123027481392741907)
XLA Ops:
  0.6 0.0 copy-start.4
  0.6 0.7 copy-done.4
  1.3 0.7 copy.14.sel_ref
  2.0 1.3 %copy_bitcast_fusion.2 = (bf16[1,512,4,128]{3,1,0,2:T(8,128)(2,1)S(1)}, bf16[1,512,4,128]{3,1,0,2:T(8,128)(2,1)S(1)}) fusion(bf16[512,4,128]{2,1,0:T(4,128)(2,1)} %param.7, bf16[512,4,128]{2,1,0:T(4,128)(2,1)} %param.6), kind=kLoop, calls=%fused_computation.5 | loop fusion | bytes 2097152 | tf_op jit(solution)/shard_map/stack | solution.py:449
  3.3 0.9 fusion.2.own_ref
  4.2 0.0 copy-start.1
  4.2 0.0 copy-start.2
  4.2 0.1 fusion
  4.3 0.8 copy.11
  5.1 0.5 copy-done.1
  5.6 0.3 copy-done.2
  5.9 1.7 %copy_bitcast_fusion = (bf16[4,2,512,128]{3,2,1,0:T(8,128)(2,1)}, bf16[4,2,512,128]{3,2,1,0:T(8,128)(2,1)}) fusion(bf16[512,2,4,128]{3,2,1,0:T(4,128)(2,1)S(1)} %copy-done.1, bf16[512,2,4,128]{3,2,1,0:T(4,128)(2,1)S(1)} %copy-done.2), kind=kLoop, calls=%fused_computation.2 | loop fusion | bytes 4194304 | tf_op jit(solution)/shard_map/transpose | solution.py:454
  7.6 79.6 %shard_map.84 = (bf16[4,8,64,128]{3,2,1,0:T(8,128)(2,1)}, bf16[4,2,512,128]{3,2,1,0:T(8,128)(2,1)}, bf16[4,2,512,128]{3,2,1,0:T(8,128)(2,1)}) custom-call(s32[16,2]{1,0:T(8,128)} %copy.14.sel_ref, bf16[4,8,64,128]{3,2,1,0:T(8,128)(2,1)} %bitcast.23, bf16[2,2,512,128]{3,2,1,0:T(8,128)(2,1)} %fusion.2.own_ref, ...), custom_call_target="tpu_custom_call" | custom-call | tf_op jit(solution)/shard_map/pallas_call | solution.py:401
  87.2 0.0 copy-start
  87.2 3.1 %copy.17 = bf16[512,2,4,128]{3,2,1,0:T(4,128)(2,1)} copy(bf16[512,2,4,128]{3,0,1,2:T(8,128)(2,1)} %bitcast.25) | data formatting | bytes 2097152
  90.3 0.0 copy-done
  90.3 0.0 copy-start.3
  90.3 1.8 %copy.18 = bf16[512,2,4,128]{3,2,1,0:T(4,128)(2,1)} copy(bf16[512,2,4,128]{3,0,1,2:T(8,128)(2,1)S(1)} %bitcast.24) | data formatting | bytes 2097152
  92.1 0.0 copy-done.3
  92.2 1.0 %copy.16 = bf16[1,2,256,2,128]{4,3,2,1,0:T(2,128)(2,1)} copy(bf16[1,2,256,2,128]{4,2,0,1,3:T(8,128)(2,1)S(1)} %get-tuple-element.14) | data formatting | bytes 524288 | tf_op jit(solution)/shard_map/slice | solution.py:458
  93.1 1.0 %copy.15 = bf16[1,2,256,2,128]{4,3,2,1,0:T(2,128)(2,1)} copy(bf16[1,2,256,2,128]{4,2,0,1,3:T(8,128)(2,1)S(1)} %get-tuple-element.15) | data formatting | bytes 524288 | tf_op jit(solution)/shard_map/slice | solution.py:458
  (1 shorter events, 0.0 us)
Async XLA Ops:
  0.6 0.7 copy-start.4
  4.2 1.4 %copy-start.1 = (bf16[512,2,4,128]{3,2,1,0:T(4,128)(2,1)S(1)}, bf16[512,2,4,128]{3,2,1,0:T(4,128)(2,1)}, u32[]{:S(2)}) copy-start(bf16[512,2,4,128]{3,2,1,0:T(4,128)(2,1)} %param.8) | copy-start | bytes 3145732
  4.2 1.7 %copy-start.2 = (bf16[512,2,4,128]{3,2,1,0:T(4,128)(2,1)S(1)}, bf16[512,2,4,128]{3,2,1,0:T(4,128)(2,1)}, u32[]{:S(2)}) copy-start(bf16[512,2,4,128]{3,2,1,0:T(4,128)(2,1)} %param.5) | copy-start | bytes 3145732
  87.2 3.1 %copy-start = (bf16[4,2,512,128]{3,2,1,0:T(8,128)(2,1)S(1)}, bf16[4,2,512,128]{3,2,1,0:T(8,128)(2,1)}, u32[]{:S(2)}) copy-start(bf16[4,2,512,128]{3,2,1,0:T(8,128)(2,1)} %get-tuple-element.8) | copy-start | bytes 3145732
  90.3 1.8 %copy-start.3 = (bf16[4,8,64,128]{3,2,1,0:T(8,128)(2,1)S(1)}, bf16[4,8,64,128]{3,2,1,0:T(8,128)(2,1)}, u32[]{:S(2)}) copy-start(bf16[4,8,64,128]{3,2,1,0:T(8,128)(2,1)} %get-tuple-element.9) | copy-start | bytes 1572868

commit v2 on v1

--- a/solution.py
+++ b/solution.py
@@ -11,6 +11,8 @@
 F32 = jnp.float32
 BF16 = jnp.bfloat16
 CHUNKS = 2
+EXTRA = 16
+TILE = 256
 
 
 def dot_nn(a, b):
@@ -27,17 +29,29 @@
 
     for i in range(1, halves):
         pl.semaphore_signal(barrier, inc=1, device_id={"ctx": me, "head": lax.rem(half + i, halves)})
-    pl.semaphore_wait(barrier, blocks - 1 + halves - 1)
+    return lambda: pl.semaphore_wait(barrier, blocks - 1 + halves - 1)
+
+
+def pick(shape, column_of):
+    row = lax.broadcasted_iota(jnp.int32, shape, 0)
+    column = lax.broadcasted_iota(jnp.int32, shape, 1)
+    return jnp.where(column == column_of(row), 1.0, 0.0).astype(BF16)
+
+
+def split(x, size):
+    bits = size.bit_length() - 1
+    assert size == 1 << bits
+    return lax.shift_right_logical(x, bits), lax.bitwise_and(x, size - 1)
 
 
 def flip(x):
     return x.astype(F32).T.astype(BF16)
 
 
-def step_kernel(blocks, halves, sel_ref, kv_ref, own_ref, q_ref, do_ref, grads_ref, oo_ref, dqo_ref,
-                qv, dov, qt, dot, near, send, ks, vs, kt, vt, probs, dots, dqt, dk, dv, dko, dvo, down, outv, dqv,
+def step_kernel(blocks, halves, sel_ref, k_ref, v_ref, q_ref, do_ref, oo_ref, dqo_ref, gk_ref, gv_ref,
+                kv_raw, raw, staged, own_ref, kv_ref, perm, back, qv, dov, qt, dot, near, send, ks, vs, kt, vt, marks, peaks, probs, dots, dqt, dk, dv, dko, dvo, down, outv, dqv, landed,
                 dnear, arrived, home, ret,
-                s1, r1, s2, r2, xs, xr, xl, b1, c1, b2, c2, ys, yr, yl, *held):
+                s1, r1, s2, r2, kl, ql, ol, xs, xr, xl, b1, c1, b2, c2, ys, yr, yl, *held):
     me, half = lax.axis_index("ctx"), lax.axis_index("head")
     heads, group, rows, size = qv.shape
     part = group // halves
@@ -50,9 +64,59 @@
     lower, upper = side == 0, side > 0
     scale = size ** -0.5
     factor = scale * math.log2(math.e)
-    visible = [sel_ref[me, j] < me for j in range(2)]
+    visible = [sel_ref[j, me] < me for j in range(2)]
     here = {"ctx": me, "head": half}
-    greet(blocks, halves)
+    kv_heads = staged.shape[1]
+    joined = greet(blocks, halves)
+
+    loads = [pltpu.make_async_copy(src, kv_raw.at[e], kl.at[e]) for e, src in enumerate((k_ref, v_ref))]
+    reads = [pltpu.make_async_copy(src, raw.at[e], ql.at[e]) for e, src in enumerate((q_ref, do_ref))]
+    for copy in loads + reads:
+        copy.start()
+
+    kv_tokens = TILE // kv_heads
+    tokens = TILE // (kv_heads * part)
+    grad_tokens = TILE // heads
+
+    def kv_column(row):
+        h, t = split(row, kv_tokens)
+        return t * kv_heads + half * heads + h
+
+    def q_column(row):
+        slab, t = split(row, tokens)
+        n, g = split(slab, part)
+        return t * (part * kv_heads) + g * kv_heads + n
+
+    def q_back(row):
+        t, slab = split(row, part * kv_heads)
+        g, n = split(slab, kv_heads)
+        return (n * part + g) * tokens + t
+
+    def grad_back(row):
+        t, h = split(row, heads)
+        return h * grad_tokens + t
+
+    choose = pick((heads * kv_tokens, TILE), kv_column)
+    vt[:, size:size + EXTRA, :] = jnp.ones((heads, EXTRA, 3 * rows), BF16)
+    for copy in loads:
+        copy.wait()
+    for e in range(2):
+        for i in range(rows // kv_tokens):
+            y = dot_nn(choose, kv_raw[e, i * TILE:(i + 1) * TILE, :]).astype(BF16)
+            for h in range(heads):
+                own_ref[h, e, i * kv_tokens:(i + 1) * kv_tokens] = y[h * kv_tokens:(h + 1) * kv_tokens]
+    pieces = side_blocks // 2
+
+    def cut(x):
+        if piece % 16 == 0:
+            return x.reshape(pieces, piece, size)
+        return x.astype(F32).reshape(pieces, piece, size).astype(BF16)
+
+    for n in range(heads):
+        for k in range(CHUNKS):
+            for e in range(2):
+                kv_ref[n * CHUNKS + k, e * pieces:(e + 1) * pieces] = cut(own_ref[n, e, k * keys:(k + 1) * keys])
+    joined()
 
     def near_all(make):
         @pl.loop(1, side_blocks)
@@ -75,8 +139,25 @@
 
         near_all(scatter(u, base))
 
+    perm[...] = pick((TILE, TILE), q_column)
+    back[0] = pick((TILE, TILE), q_back)
+    back[1] = pick((TILE, TILE), grad_back)
+    for copy in reads:
+        copy.wait()
+
+    @pl.loop(0, rows // tokens)
+    def _(i):
+        at = pl.multiple_of(i * tokens, tokens)
+        for e in range(2):
+            y = dot_nn(perm[...], raw[e, pl.ds(pl.multiple_of(i * TILE, TILE), TILE), :]).astype(BF16)
+            for n in range(kv_heads):
+                for g in range(part):
+                    slab = (n * part + g) * tokens
+                    staged[e, n, g, pl.ds(at, tokens), :] = y[slab:slab + tokens]
+
     moves = []
-    for e, (src, dst) in enumerate(((q_ref, qv), (do_ref, dov))):
+    for e, dst in enumerate((qv, dov)):
+        src = staged.at[e]
         place = dst.at[:, pl.ds(half * part, part)]
         for i in range(1, halves):
             other = lax.rem(half + i, halves)
@@ -111,12 +192,12 @@
         @pl.loop(0, side_blocks)
         def _(d):
             for j in range(2):
-                send[u, d, j] = held[u][sel_ref[base + d, j]]
+                send[u, d, j] = held[u][sel_ref[j, base + d]]
 
         near_all(lambda d: pltpu.make_async_remote_copy(
             send.at[u, d], near.at[u, :, col], s2.at[u], r2.at[u], device_id={"ctx": base + d, "head": half}))
         for j in range(2):
-            near[u, j, col] = held[u][sel_ref[me, j]]
+            near[u, j, col] = held[u][sel_ref[j, me]]
 
     def back_first(u):
         span = pl.ds(0, side_blocks - 1)
@@ -139,7 +220,7 @@
                     d = c * together + k
                     b = base + d
                     for j in range(2):
-                        mine = ((sel_ref[b, j] == s) & (b > s)).astype(F32)
+                        mine = ((sel_ref[j, b] == s) & (b > s)).astype(F32)
                         total = total + arrived[u, d, j].astype(F32) * mine
                 return total
 
@@ -175,7 +256,7 @@
         ret[u, side, col] = home[u, me]
 
     def results(n, e):
-        src, dst = ((outv, oo_ref), (dqv, dqo_ref))[e]
+        src, dst = (outv, dqv)[e], landed.at[e]
         made = []
         place = dst.at[half * heads + n]
         for i in range(1, halves):
@@ -191,47 +272,52 @@
             return x.reshape(keys, size)
         return x.astype(F32).reshape(keys, size).astype(BF16)
 
-    pieces = side_blocks // 2
-
     def place_keys(n, j, k, key, value):
         ks[n, j, k * keys:(k + 1) * keys] = key
         vs[n, j, k * keys:(k + 1) * keys] = value
         kt[n, j, k] = flip(key)
-        vt[n, :, j * rows + k * keys:j * rows + (k + 1) * keys] = flip(value)
-
-    def outputs(n, g):
+        vt[n, 0:size, j * rows + k * keys:j * rows + (k + 1) * keys] = flip(value)
+
+    def cuts_of(t):
+        return ([(j, at) for j in range(2) for at in range(0, rows, tile)]
+                + [(2, at) for at in range(0, (t + 1) * tile, tile)])
+
+    def score(n, g):
+        for t in range(2):
+            q_t = qt[n, g, :, t * tile:(t + 1) * tile]
+            tops = [None] * 3
+            for j, at in cuts_of(t):
+                s = dot_nn(ks[n, j, at:at + tile, :], q_t)
+                if j == 2 and at == t * tile:
+                    key_at = lax.broadcasted_iota(jnp.int32, s.shape, 0)
+                    query_at = lax.broadcasted_iota(jnp.int32, s.shape, 1)
+                    s = jnp.where(key_at <= query_at, s, -jnp.inf)
+                marks[t, j * rows + at:j * rows + at + tile, :] = s
+                top = jnp.max(s, axis=0, keepdims=True)
+                tops[j] = top if tops[j] is None else jnp.maximum(tops[j], top)
+            top = tops[2]
+            for j in range(2):
+                top = jnp.maximum(top, jnp.where(visible[j], tops[j], -jnp.inf))
+            peaks[t] = top * factor
+
+    def weigh(n, g):
         for t in range(2):
             span = slice(t * tile, (t + 1) * tile)
-            counts = (rows, rows, (t + 1) * tile)
-            q_t = qt[n, g, :, span]
-            scores, tops = [], []
-            for j in range(3):
-                s = dot_nn(ks[n, j, 0:counts[j], :], q_t) * factor
-                if j == 2:
-                    key_at = lax.broadcasted_iota(jnp.int32, s.shape, 0)
-                    query_at = lax.broadcasted_iota(jnp.int32, s.shape, 1) + t * tile
-                    s = jnp.where(key_at <= query_at, s, -jnp.inf)
-                top = jnp.max(s, axis=0, keepdims=True)
-                if j < 2:
-                    top = jnp.where(visible[j], top, -jnp.inf)
-                scores.append(s)
-                tops.append(top)
-            top = jnp.maximum(jnp.maximum(tops[0], tops[1]), tops[2])
-            total = jnp.zeros_like(top)
-            weights = []
-            for j in range(3):
-                shift = jnp.where(visible[j], top, jnp.inf) if j < 2 else top
-                e = jnp.exp2(scores[j] - shift)
-                total = total + jnp.sum(e, axis=0, keepdims=True)
-                weights.append(e)
-            inverse = 1.0 / total
-            out_t = jnp.zeros((size, tile), F32)
-            for j in range(3):
-                low = (weights[j] * inverse).astype(BF16)
-                probs[n, g, j * rows:j * rows + counts[j], span] = low
-                out_t = out_t + dot_nn(vt[n, :, j * rows:j * rows + counts[j]], low)
-            out_low = out_t.astype(BF16).astype(F32)
-            dots[n, g, :, span] = jnp.sum(dot[n, g, :, span].astype(F32) * out_low, axis=0, keepdims=True)
+            top = peaks[t]
+            shifts = [jnp.where(visible[j], top, jnp.inf) for j in range(2)] + [top]
+            out_t = jnp.zeros((size + EXTRA, tile), F32)
+            for j, at in cuts_of(t):
+                span_k = slice(j * rows + at, j * rows + at + tile)
+                low = jnp.exp2(marks[t, span_k, :] * factor - shifts[j]).astype(BF16)
+                probs[n, g, span_k, span] = low
+                out_t = out_t + dot_nn(vt[n, :, span_k], low)
+            inverse = 1.0 / out_t[size:size + 1]
+            out_low = (out_t[0:size] * inverse).astype(BF16).astype(F32)
+            do_low = (dot[n, g, :, span].astype(F32) * inverse).astype(BF16)
+            do_wide = do_low.astype(F32)
+            dot[n, g, :, span] = do_low
+            dov[n, g, span, :] = do_wide.T.astype(BF16)
+            dots[n, g, :, span] = jnp.sum(do_wide * out_low, axis=0, keepdims=True)
             outv[n, g, span, :] = out_low.T.astype(BF16)
 
     def gradients(n, g, low, key_t, value, span, dk_at, dv_at):
@@ -298,16 +384,25 @@
             for j in range(2):
                 place_keys(n, j, k, join(near[u, j, 0:pieces]), join(near[u, j, pieces:2 * pieces]))
 
-        @pl.loop(0, group)
-        def _(g):
-            outputs(n, g)
+        @pl.loop(0, 2 * group)
+        def _(at):
+            g = at // 2
+
+            @pl.when(lax.rem(at, 2) == 0)
+            def _():
+                score(n, g)
+
+            @pl.when(lax.rem(at, 2) == 1)
+            def _():
+                weigh(n, g)
+
             for m in range(1, heads):
                 for k in range(CHUNKS):
-                    @pl.when((n == m - 1) & (g == k * (group - 1)))
+                    @pl.when((n == m - 1) & (at == 1 + 2 * k * (group - 1)))
                     def _(m=m, k=k):
                         relay(m * CHUNKS + k)
 
-            @pl.when((n > 0) & (lax.rem(g, 2) == 1))
+            @pl.when((n > 0) & (lax.rem(at, 4) == 3))
             def _():
                 collect((n - 1) * CHUNKS + g // 2)
 
@@ -363,48 +458,90 @@
             for move in results(n, 1):
                 move.start()
 
+    writes = []
+    for e, dst in enumerate((oo_ref, dqo_ref)):
+        for n in range(heads):
+            for move in results(n, e):
+                move.wait()
+
+        @pl.loop(0, rows // tokens)
+        def _(i, e=e):
+            at = pl.multiple_of(i * tokens, tokens)
+            x = jnp.concatenate([landed[e, n, g, pl.ds(at, tokens), :]
+                                 for n in range(kv_heads) for g in range(part)], axis=0)
+            raw[e, pl.ds(pl.multiple_of(i * TILE, TILE), TILE), :] = dot_nn(back[0], x).astype(BF16)
+
+        writes.append(pltpu.make_async_copy(raw.at[e], dst, ol.at[e]))
+        writes[e].start()
+
     for u in range(units):
         fetch_last(u).wait_send()
         back_first(u).wait_send()
-    for n in range(heads):
-        for e in range(2):
-            for move in results(n, e):
-                move.wait()
+
+    def finish(k, low):
+        for e, dst in enumerate((gk_ref, gv_ref)):
+            span = slice(e * pieces, (e + 1) * pieces)
+            parts = []
+            for n in range(heads):
+                u = n * CHUNKS + k
+                total = down[u, span] + ret[u, 1, span].astype(F32)
+                if low:
+                    total = total + ret[u, 0, span].astype(F32)
+                parts.append(total.reshape(keys, size).astype(BF16))
+            for i in range(keys // grad_tokens):
+                x = jnp.concatenate([p[i * grad_tokens:(i + 1) * grad_tokens] for p in parts], axis=0)
+                at = k * keys * heads + i * TILE
+                dst[at:at + TILE, :] = dot_nn(back[1], x).astype(BF16)
 
     @pl.when(lower)
     def _():
         for u in range(units):
             fetch_first(u, blocks - 1).wait_send()
             back_last(u, side_blocks - 1).wait_send()
-            back_last(u, blocks - 1).wait_recv()
-            grads_ref[u] = (ret[u, 1].astype(F32) + ret[u, 0].astype(F32) + down[u]).astype(BF16)
+        for k in range(CHUNKS):
+            for n in range(heads):
+                back_last(n * CHUNKS + k, blocks - 1).wait_recv()
+            finish(k, True)
 
     @pl.when(upper)
     def _():
         for u in range(units):
             fetch_first(u, side_blocks - 1).wait_send()
             back_last(u, blocks - 1).wait_send()
-            back_last(u, side_blocks - 1).wait_recv()
-            grads_ref[u] = (ret[u, 1].astype(F32) + down[u]).astype(BF16)
-
-
-def step(selected, kv, own, q, do, blocks, halves):
-    units, side_blocks, piece, size = kv.shape
-    heads = units // CHUNKS
-    full, part, rows, _ = q.shape
-    group = part * halves
-    keys = rows // CHUNKS
+        for k in range(CHUNKS):
+            for n in range(heads):
+                back_last(n * CHUNKS + k, side_blocks - 1).wait_recv()
+            finish(k, False)
+
+    for write in writes:
+        write.wait()
+
+
+def step(selected, key, value, q, do, blocks, halves, rows, part):
+    size = key.shape[1]
+    kv_heads = key.shape[0] // rows
+    heads, group = kv_heads // halves, part * halves
+    units, side_blocks, keys = heads * CHUNKS, blocks // 2, rows // CHUNKS
+    piece = 2 * keys // side_blocks
     near = pl.BlockSpec(memory_space=pltpu.VMEM)
     far = pl.BlockSpec(memory_space=pl.ANY)
     dma = pltpu.SemaphoreType.DMA
     vmem = pltpu.VMEM
+    wide = jax.ShapeDtypeStruct(q.shape, BF16)
+    grad = jax.ShapeDtypeStruct((rows * heads, size), BF16)
     return pl.pallas_call(
         functools.partial(step_kernel, blocks, halves),
-        in_specs=[pl.BlockSpec(memory_space=pltpu.SMEM), near, near, far, far],
-        out_specs=[near, far, far],
-        out_shape=[jax.ShapeDtypeStruct(kv.shape, BF16), jax.ShapeDtypeStruct(q.shape, BF16),
-                   jax.ShapeDtypeStruct(q.shape, BF16)],
+        in_specs=[pl.BlockSpec(memory_space=pltpu.SMEM), far, far, far, far],
+        out_specs=[far, far, near, near],
+        out_shape=[wide, wide, grad, grad],
         scratch_shapes=[
+            vmem((2,) + key.shape, BF16),
+            vmem((2,) + q.shape, BF16),
+            vmem((2, kv_heads, part, rows, size), BF16),
+            vmem((heads, 2, rows, size), BF16),
+            vmem((units, side_blocks, piece, size), BF16),
+            vmem((TILE, TILE), BF16),
+            vmem((2, TILE, TILE), BF16),
             vmem((heads, group, rows, size), BF16),
             vmem((heads, group, rows, size), BF16),
             vmem((heads, group, size, rows), BF16),
@@ -414,7 +551,9 @@
             vmem((heads, 3, rows, size), BF16),
             vmem((heads, 3, rows, size), BF16),
             vmem((heads, 3, CHUNKS, size, keys), BF16),
-            vmem((heads, size, 3 * rows), BF16),
+            vmem((heads, size + EXTRA, 3 * rows), BF16),
+            vmem((2, 3 * rows, rows // 2), F32),
+            vmem((2, 1, rows // 2), F32),
             vmem((heads, group, 3 * rows, rows), BF16),
             vmem((heads, group, 1, rows), F32),
             vmem((heads, group, size, rows), F32),
@@ -425,37 +564,29 @@
             vmem((units, side_blocks, piece, size), F32),
             vmem((heads, group, rows, size), BF16),
             vmem((heads, group, rows, size), BF16),
+            vmem((2, kv_heads, part, rows, size), BF16),
             vmem((units, 2, side_blocks, piece, size), BF16),
             vmem((units, side_blocks, 2, piece, size), BF16),
             vmem((units, blocks, piece, size), BF16),
             vmem((units, 2, side_blocks, piece, size), BF16),
             dma((units,)), dma((units,)), dma((units,)), dma((units,)),
-            dma((2, halves - 1)), dma((2, halves - 1)), dma((2,)),
+            dma((2,)), dma((2,)), dma((2,)), dma((2, halves - 1)), dma((2, halves - 1)), dma((2,)),
             dma((units,)), dma((units,)), dma((units,)), dma((units,)),
             dma((heads, 2, halves - 1)), dma((heads, 2, halves - 1)), dma((heads, 2)),
         ] + [vmem((blocks, piece, size), BF16)] * units,
         compiler_params=pltpu.CompilerParams(collective_id=0, has_side_effects=True,
                                              vmem_limit_bytes=56 * 2**20),
-    )(selected, kv, own, q, do)
+    )(selected, key, value, q, do)
 
 
 def on_device(queries, keys, values, output_gradient, selected):
     rows, kv_count, size = keys.shape
     blocks, halves = lax.axis_size("ctx"), lax.axis_size("head")
-    own_heads = kv_count // halves
-    half = lax.axis_index("head")
-    side_blocks = blocks // 2
-    piece = 2 * rows // (CHUNKS * side_blocks)
-    own = jnp.stack([keys, values])
-    own = lax.dynamic_slice_in_dim(own, half * own_heads, own_heads, 2)
-    own = jnp.transpose(own, (2, 0, 1, 3))
-    cut = own.reshape(own_heads, 2, CHUNKS, rows // CHUNKS, size)
-    cut = jnp.transpose(cut, (0, 2, 1, 3, 4)).reshape(own_heads * CHUNKS, side_blocks, piece, size)
-    q, do = jnp.transpose(queries, (2, 1, 0, 3)), jnp.transpose(output_gradient, (2, 1, 0, 3))
-    grads, out, dq = step(selected, cut, own, q, do, blocks, halves)
-    grads = grads.reshape(own_heads, CHUNKS, 2, rows // CHUNKS, size)
-    grads = jnp.transpose(grads, (2, 1, 3, 0, 4)).reshape(2, rows, own_heads, size)
-    return jnp.transpose(out, (2, 1, 0, 3)), jnp.transpose(dq, (2, 1, 0, 3)), grads[0], grads[1]
+    part = queries.shape[1]
+    flat = [x.reshape(-1, size) for x in (keys, values, queries, output_gradient)]
+    out, dq, gk, gv = step(selected.T, *flat, blocks, halves, rows, part)
+    own = (rows, kv_count // halves, size)
+    return out.reshape(queries.shape), dq.reshape(queries.shape), gk.reshape(own), gv.reshape(own)
 
 
 def solution(mesh):

time: 94.4 us -> 82.9 us (0.88)
  local copies, waits for them, and re-layouts: 12.9 us -> 5.48 us
  Pallas kernels: 79.6 us -> 76.5 us
    pallas_call x1, Pallas kernels: 79.6 us -> 76.5 us  [step(): pl.pallas_call(functools.partial(step_kernel, blocks, halves), in_specs=[...]
    transpose x2 -> x0, local copies, waits for them, and re-layouts: 2.54 us -> none  [the longest x1 1.69 us: on_device(): jnp.transpose(output_gradient, (2, 1, 0, 3))]
    slice x3 -> x0, local copies, waits for them, and re-layouts: 1.98 us -> none  [the longest x2 1.01 us: on_device(): grads[1]]
    unnamed x13 -> x10, local copies, waits for them, and re-layouts: 7.06 us -> 5.48 us
    another operation x1 -> x0, local copies, waits for them, and re-layouts: 1.34 us -> none  [on_device(): own = jnp.stack([keys, values])]
where the time goes in v2:
time: 82.9 us; the launch traced here: 82.7 us
  Pallas kernels  76.5 us (92%)
  local copies, waits for them, and re-layouts  5.48 us (7%)
    pallas_call x1, Pallas kernels, step(): pl.pallas_call(functools.partial(step_kernel, blocks, halves), in_specs=[...  76.5 us
    unnamed x10, local copies, waits for them, and re-layouts  5.48 us

profile of v2, /device:TPU:0, one launch (start us, length us, event | category | flops | bytes accessed | tf_op | source)
XLA Modules:
  0.0 82.7 jit_solution(954704929479400337)
XLA Ops:
  0.6 76.5 %shard_map.84 = (bf16[4096,128]{1,0:T(8,128)(2,1)}, bf16[4096,128]{1,0:T(8,128)(2,1)}, bf16[1024,128]{1,0:T(8,128)(2,1)}, bf16[1024,128]{1,0:T(8,128)(2,1)}) custom-call(s32[2,16]{1,0:T(2,128)} %bitcast.17, bf16[2048,128]{1,0:T(8,128)(2,1)} %bitcast.13, bf16[2048,128]{1,0:T(8,128)(2,1)} %bitcast.14, bf16[4096,128]{1,0:T(8,128)(2,1)} %bitcast.9, ...), custom_call_target="tpu_custom_call" | custom-call | tf_op jit(solution)/shard_map/pallas_call | solution.py:532
  77.2 0.0 copy-start
  77.2 2.6 %copy.13 = bf16[512,2,4,128]{3,2,1,0:T(4,128)(2,1)} copy(bf16[512,2,4,128]{3,2,1,0:T(4,128)(2,1)} %bitcast.12) | data formatting | bytes 2097152
  79.8 0.0 copy-done
  79.8 0.0 copy-start.2
  79.8 1.0 %copy.14 = bf16[512,2,4,128]{3,2,1,0:T(4,128)(2,1)} copy(bf16[512,2,4,128]{3,2,1,0:T(4,128)(2,1)S(1)} %bitcast.11) | data formatting | bytes 2097152
  80.8 0.1 copy-done.2
  80.9 0.0 copy-start.1
  80.9 0.7 copy.15
  81.6 0.3 copy-done.1
  82.0 0.7 copy.16
Async XLA Ops:
  77.2 2.7 %copy-start = (bf16[4096,128]{1,0:T(8,128)(2,1)S(1)}, bf16[4096,128]{1,0:T(8,128)(2,1)}, u32[]{:S(2)}) copy-start(bf16[4096,128]{1,0:T(8,128)(2,1)} %get-tuple-element.9) | copy-start | bytes 3145732
  79.8 1.1 %copy-start.2 = (bf16[1024,128]{1,0:T(8,128)(2,1)S(1)}, bf16[1024,128]{1,0:T(8,128)(2,1)}, u32[]{:S(2)}) copy-start(bf16[1024,128]{1,0:T(8,128)(2,1)} %get-tuple-element.10) | copy-start | bytes 786436
  80.9 1.0 %copy-start.1 = (bf16[1024,128]{1,0:T(8,128)(2,1)S(1)}, bf16[1024,128]{1,0:T(8,128)(2,1)}, u32[]{:S(2)}) copy-start(bf16[1024,128]{1,0:T(8,128)(2,1)} %get-tuple-element.11) | copy-start | bytes 786436

commit v3 on v2

--- a/solution.py
+++ b/solution.py
@@ -13,6 +13,7 @@
 CHUNKS = 2
 EXTRA = 16
 TILE = 256
+PARTS = 4
 
 
 def dot_nn(a, b):
@@ -133,11 +134,11 @@
             kv_ref.at[u, d], held[u].at[me], s1.at[u], r1.at[u], device_id={"ctx": first + d, "head": half})
 
     for u in range(units):
+        near_all(scatter(u, base))
+
         @pl.when(lower)
         def _(u=u):
             far_all(scatter(u, side_blocks))
-
-        near_all(scatter(u, base))
 
     perm[...] = pick((TILE, TILE), q_column)
     back[0] = pick((TILE, TILE), q_back)
@@ -579,12 +580,46 @@
     )(selected, key, value, q, do)
 
 
+def hand_out_kernel(*refs):
+    count = (len(refs) - 2) // 3
+    sources, targets, held = refs[:count], refs[count:2 * count], refs[2 * count:3 * count]
+    into, out = refs[3 * count:]
+    pieces = []
+    for e in range(count):
+        step_rows = held[e].shape[0] // PARTS
+        for p in range(PARTS):
+            span = pl.ds(p * step_rows, step_rows)
+            pieces.append((pltpu.make_async_copy(sources[e].at[span], held[e].at[span], into.at[e, p]),
+                           pltpu.make_async_copy(held[e].at[span], targets[e].at[span], out.at[e, p])))
+    for first, _ in pieces:
+        first.start()
+    for first, second in pieces:
+        first.wait()
+        second.start()
+    for _, second in pieces:
+        second.wait()
+
+
+def hand_out(arrays):
+    far = pl.BlockSpec(memory_space=pl.ANY)
+    count = len(arrays)
+    return pl.pallas_call(
+        hand_out_kernel,
+        in_specs=[far] * count,
+        out_specs=[far] * count,
+        out_shape=[jax.ShapeDtypeStruct(x.shape, x.dtype) for x in arrays],
+        scratch_shapes=[pltpu.VMEM(x.shape, x.dtype) for x in arrays]
+        + [pltpu.SemaphoreType.DMA((count, PARTS))] * 2,
+        compiler_params=pltpu.CompilerParams(vmem_limit_bytes=60 * 2**20),
+    )(*arrays)
+
+
 def on_device(queries, keys, values, output_gradient, selected):
     rows, kv_count, size = keys.shape
     blocks, halves = lax.axis_size("ctx"), lax.axis_size("head")
     part = queries.shape[1]
     flat = [x.reshape(-1, size) for x in (keys, values, queries, output_gradient)]
-    out, dq, gk, gv = step(selected.T, *flat, blocks, halves, rows, part)
+    out, dq, gk, gv = hand_out(step(selected.T, *flat, blocks, halves, rows, part))
     own = (rows, kv_count // halves, size)
     return out.reshape(queries.shape), dq.reshape(queries.shape), gk.reshape(own), gv.reshape(own)
 

time: 82.9 us -> 79.8 us (0.963)
  local copies, waits for them, and re-layouts: 5.48 us -> 0 us
  Pallas kernels: 76.5 us -> 78.9 us
    unnamed x10 -> x0, local copies, waits for them, and re-layouts: 5.48 us -> none
    pallas_call x0 -> x1, Pallas kernels: none -> 2.7 us  [hand_out(): pl.pallas_call(hand_out_kernel, in_specs=[far] * count, out_specs=[far] *...]
where the time goes in v3:
time: 79.8 us; the launch traced here: 79.6 us
  Pallas kernels  78.9 us (99%)
    pallas_call x1, Pallas kernels, step(): pl.pallas_call(functools.partial(step_kernel, blocks, halves), in_specs=[...  76.2 us
    pallas_call x1, Pallas kernels, hand_out(): pl.pallas_call(hand_out_kernel, in_specs=[far] * count, out_specs=[far] *...  2.7 us

profile of v3, /device:TPU:0, one launch (start us, length us, event | category | flops | bytes accessed | tf_op | source)
XLA Modules:
  0.0 79.6 jit_solution(216712740061871297)
XLA Ops:
  0.6 76.2 %shard_map.84 = (bf16[4096,128]{1,0:T(8,128)(2,1)}, bf16[4096,128]{1,0:T(8,128)(2,1)}, bf16[1024,128]{1,0:T(8,128)(2,1)}, bf16[1024,128]{1,0:T(8,128)(2,1)}) custom-call(s32[2,16]{1,0:T(2,128)} %bitcast.13, bf16[2048,128]{1,0:T(8,128)(2,1)} %bitcast.11, bf16[2048,128]{1,0:T(8,128)(2,1)} %bitcast.12, bf16[4096,128]{1,0:T(8,128)(2,1)} %bitcast.9, ...), custom_call_target="tpu_custom_call" | custom-call | tf_op jit(solution)/shard_map/pallas_call | solution.py:533
  76.9 2.7 %shard_map.85 = (bf16[4096,128]{1,0:T(8,128)(2,1)}, bf16[4096,128]{1,0:T(8,128)(2,1)}, bf16[1024,128]{1,0:T(8,128)(2,1)}, bf16[1024,128]{1,0:T(8,128)(2,1)}) custom-call(bf16[4096,128]{1,0:T(8,128)(2,1)} %get-tuple-element.12.refs_0_, bf16[4096,128]{1,0:T(8,128)(2,1)} %get-tuple-element.13.refs_1_, bf16[1024,128]{1,0:T(8,128)(2,1)} %get-tuple-element.14.refs_2_, ...), custom_call_target="tpu_custom_call" | custom-call | tf_op jit(solution)/shard_map/pallas_call | solution.py:606
